TPU v7x, 32 devices: a whole 2x2x4 slice. The times are simulated.
32 devices in a mesh: groups: 2 (over y), ctx: 4 (over z), head: 2 (over x), tp: 2 (over core).
Axes of the slice: x: 2, y: 2, z: 4, core: 2. Of those that a mesh axis runs over, the one named last changes fastest.
Arguments:
- queries: bfloat16 [32, 2048, 128], P(('head', 'tp'), ('groups', 'ctx')), parts along dimension 1, may hold values from -80 to 80
- stretch_keys: bfloat16 [8, 2048, 128], P(('head', 'tp'), ('groups', 'ctx')), parts along dimension 1, may hold values from -120 to 120
- stretch_values: bfloat16 [8, 2048, 128], P(('head', 'tp'), ('groups', 'ctx')), parts along dimension 1, may hold values from -6 to 6
- cache_keys: bfloat16 [8, 32768, 128], P(('head', 'tp'), ('groups', 'ctx')), parts along dimension 1, may hold values from -6 to 6
- cache_values: bfloat16 [8, 32768, 128], P(('head', 'tp'), ('groups', 'ctx')), parts along dimension 1, may hold values from -6 to 6
- block_picks: int32 [4, 8, 16], P('groups'), parts along dimension 0, may hold values from 0 to 31, as said below
- block_table: int32 [64], P('groups'), parts along dimension 0, may hold values from 0 to 31, as said below
Outputs:
- attended: bfloat16 [32, 2048, 128], P(('head', 'tp'), ('groups', 'ctx')), parts along dimension 1
There are 2 independent parts, one for each index of `groups`. A program takes and returns all parts, laid end to end along the dimension named above; each array names one. Nothing has to cross between parts.
Inputs may be any that keep to these rules, and one draw needn't show every extreme that they name: `block_picks`: for each query block and KV head the 16 picks are different logical blocks; exactly 4 of them have slots on each of 4 different indices of ctx, slot s lying on index s // 8. `block_table`: A permutation of the 32 physical slots.
All inputs are finite; a program needn't handle non-finite values.
Results may differ from a plain program's by a relative error of at most 0.0032.
Values may be sent and summed in bfloat16 or wider, within the bound.
No kernel may reach another device: no remote copies, remote signals or barrier semaphores. Data moves between devices by JAX's collectives and lax.ppermute only.
A program may use at most 64 MiB of HBM per device.

v0:
```python
import jax
import jax.numpy as jnp
import numpy as np
from jax import lax
from jax.sharding import PartitionSpec as P

BLOCK = 512
TOPK = 16


def shifted(value, axis, by):
    count = lax.axis_size(axis)
    pairs = [(i, i + by) for i in range(count) if 0 <= i + by < count]
    return lax.ppermute(value, axis, pairs)


def as_sent(value):

    def short(part):
        return part.astype(jnp.bfloat16) if part.dtype == jnp.float32 else part

    return jax.tree.map(short, value)


def partner(value, axis, bit):
    mask = 2**bit
    pairs = [(source, source ^ mask) for source in range(lax.axis_size(axis))]
    return lax.ppermute(value, axis, pairs)


def lookup(lookup_table, indices):
    entries = jnp.arange(lookup_table.shape[0], dtype=jnp.int32)
    return jnp.sum(jnp.where(indices[..., None] == entries, lookup_table, 0), axis=-1)


def owner_rank(owners):
    ordinal = jnp.arange(owners.shape[-1], dtype=jnp.int32)
    before = (owners[..., :, None] == owners[..., None, :]) & (ordinal[None, :] < ordinal[:, None])
    return jnp.sum(before, axis=-1)


def pick_rows(source, indices):
    return source[indices]


def take_blocks(blocks, indices):
    return jax.vmap(pick_rows)(blocks, indices)


def attend(query_rows, all_keys, all_values, allowed_mask):
    tile_relevance = jnp.einsum(
        "rd,kd->rk", query_rows, all_keys, preferred_element_type=jnp.float32
    )
    tile_relevance = tile_relevance * query_rows.shape[-1] ** (-0.5)
    tile_relevance = jnp.where(allowed_mask, tile_relevance, -jnp.inf)
    row_max = jnp.max(tile_relevance, axis=-1, keepdims=True)
    weights = jnp.exp(tile_relevance - row_max)
    weight_sum = jnp.sum(weights, axis=-1, keepdims=True)
    mixed = jnp.einsum(
        "rk,kd->rd", weights.astype(jnp.bfloat16), all_values, preferred_element_type=jnp.float32
    )
    return (mixed / weight_sum).astype(jnp.bfloat16)


def shards(
    queries, stretch_keys, stretch_values, cache_keys, cache_values, block_picks, block_table
):
    kv_dev, tok_dev, head_dim = stretch_keys.shape
    q_per_kv = queries.shape[0] // kv_dev
    blocks_dev = cache_keys.shape[1] // BLOCK
    ctx_size = lax.axis_size("ctx")
    ctx_index = lax.axis_index("ctx")
    per_peer = max(1, TOPK // ctx_size)
    parity = ctx_index % 2
    head_ids = lax.axis_index(("head", "tp")) * kv_dev + jnp.arange(kv_dev, dtype=jnp.int32)
    selector = head_ids[:, None] == jnp.arange(block_picks.shape[1], dtype=jnp.int32)[None, :]
    my_picks = jnp.sum(jnp.where(selector[None, :, :, None], block_picks[:, None, :, :], 0), axis=2)
    physical = lookup(block_table, my_picks)
    owners = physical // blocks_dev
    in_owner = physical % blocks_dev
    peer_rank = owner_rank(owners)
    targets = np.arange(ctx_size) * tok_dev // BLOCK
    target_owner = owners[targets]
    target_rank = peer_rank[targets]
    target_local = in_owner[targets]
    slot_ids = jnp.arange(per_peer, dtype=jnp.int32)
    matched = (target_owner[:, :, None, :] == ctx_index) & (
        target_rank[:, :, None, :] == slot_ids[None, None, :, None]
    )
    chosen = jnp.sum(jnp.where(matched, target_local[:, :, None, :], 0), axis=-1)
    usable = jnp.any(matched, axis=-1)
    chosen = jnp.transpose(chosen, (1, 0, 2)).reshape(kv_dev, ctx_size * per_peer)
    usable = jnp.transpose(usable, (1, 0, 2)).reshape(kv_dev, ctx_size * per_peer)
    my_block = ctx_index * tok_dev // BLOCK
    my_owner = lax.dynamic_index_in_dim(owners, my_block, 0, keepdims=False)
    my_rank = lax.dynamic_index_in_dim(peer_rank, my_block, 0, keepdims=False)
    my_slot = my_owner * per_peer + my_rank
    prev_keys, prev_values = shifted((stretch_keys, stretch_values), "ctx", 1)
    half_rows = BLOCK // 2
    key_halves = cache_keys.reshape(kv_dev, blocks_dev * 2, half_rows, head_dim)
    value_halves = cache_values.reshape(kv_dev, blocks_dev * 2, half_rows, head_dim)
    row_side = jnp.asarray(np.repeat(np.arange(ctx_size) % 2, per_peer), jnp.int32)
    half_index = chosen * 2 + row_side[None, :]
    sent_keys = jnp.where(usable[:, :, None, None], take_blocks(key_halves, half_index), 0).astype(
        jnp.bfloat16
    )
    sent_values = jnp.where(
        usable[:, :, None, None], take_blocks(value_halves, half_index), 0
    ).astype(jnp.bfloat16)
    got_keys, got_values = (
        lax.all_to_all(sent_keys, "ctx", split_axis=1, concat_axis=1, tiled=True),
        lax.all_to_all(sent_values, "ctx", split_axis=1, concat_axis=1, tiled=True),
    )
    mine_keys = take_blocks(got_keys, my_slot)
    mine_values = take_blocks(got_values, my_slot)
    other_keys, other_values = (
        partner(as_sent(mine_keys), "ctx", 0).astype(mine_keys.dtype),
        partner(as_sent(mine_values), "ctx", 0).astype(mine_values.dtype),
    )
    first_keys = jnp.where(parity == 0, mine_keys, other_keys)
    second_keys = jnp.where(parity == 0, other_keys, mine_keys)
    first_values = jnp.where(parity == 0, mine_values, other_values)
    second_values = jnp.where(parity == 0, other_values, mine_values)
    live_keys = jnp.concatenate([first_keys, second_keys], axis=2)
    live_values = jnp.concatenate([first_values, second_values], axis=2)
    span_cols = TOPK * BLOCK
    live_keys = live_keys.reshape(kv_dev, span_cols, head_dim)
    live_values = live_values.reshape(kv_dev, span_cols, head_dim)
    all_keys = jnp.concatenate([live_keys, prev_keys, stretch_keys], axis=1)
    all_values = jnp.concatenate([live_values, prev_values, stretch_values], axis=1)
    query_rows = queries.reshape(kv_dev, q_per_kv * tok_dev, head_dim)
    step_rows = min(512, q_per_kv * tok_dev)
    columns = jnp.arange(span_cols + 2 * tok_dev, dtype=jnp.int32)

    def one_head(packed):
        q_head, k_head, v_head = packed
        q_steps = q_head.reshape(-1, step_rows, head_dim)
        starts = jnp.arange(q_steps.shape[0], dtype=jnp.int32) * step_rows

        def one_step(packed_block_step):
            q_block, first_row = packed_block_step
            position = (first_row + jnp.arange(step_rows, dtype=jnp.int32)) % tok_dev
            cache_part = columns[None, :] < span_cols
            earlier_part = (
                (columns[None, :] >= span_cols)
                & (columns[None, :] < span_cols + tok_dev)
                & (columns[None, :] - span_cols > position[:, None])
                & (ctx_index > 0)
            )
            own_part = (columns[None, :] >= span_cols + tok_dev) & (
                columns[None, :] - span_cols - tok_dev <= position[:, None]
            )
            return attend(q_block, k_head, v_head, cache_part | earlier_part | own_part)

        return lax.map(one_step, (q_steps, starts)).reshape(q_per_kv * tok_dev, head_dim)

    result = lax.map(one_head, (query_rows, all_keys, all_values))
    return result.reshape(kv_dev * q_per_kv, tok_dev, head_dim)


def solution(mesh):
    placed = (
        P(("head", "tp"), ("groups", "ctx"), None),
        P(("head", "tp"), ("groups", "ctx"), None),
        P(("head", "tp"), ("groups", "ctx"), None),
        P(("head", "tp"), ("groups", "ctx"), None),
        P(("head", "tp"), ("groups", "ctx"), None),
        P("groups", None, None),
        P("groups"),
    )
    return jax.shard_map(
        shards,
        mesh=mesh,
        in_specs=placed,
        out_specs=P(("head", "tp"), ("groups", "ctx"), None),
        check_vma=False,
    )
```

profile of v0, /device:TPU:0, one launch (start us, length us, event | category | flops | bytes accessed | tf_op | source)
XLA Modules:
  0.0 363.8 jit_solution(13856905821156815247)
XLA Ops:
  0.0 0.1 iota_compare_fusion.3
  0.1 0.9 select_reduce_fusion.2
  1.0 0.9 select_reduce_fusion
  1.9 0.7 pad_clamp_fusion
  2.6 0.2 convert_reduce_fusion
  2.8 0.6 gather_fusion
  3.4 0.6 gather_fusion.1
  3.9 0.6 gather_fusion.2
  4.5 0.2 fusion.24
  4.7 0.2 select_reduce_fusion.1
  5.0 0.1 mul.65
  5.1 0.7 fusion.27
  5.7 0.1 reshape.259
  5.8 2.1 gather_fusion.3
  7.9 3.9 %gather_fusion.5 = bf16[32,256,128]{2,1,0:T(8,128)(2,1)} fusion(bf16[2,16,256,128]{3,2,1,0:T(8,128)(2,1)} %bitcast.67, s32[32]{0:T(128)S(1)} %reshape.259), kind=kCustom, calls=%fused_computation.5 | custom fusion | bytes 4194560 | tf_op jit(solution)/shard_map/vmap()/gather | solution.py:43
  11.8 0.1 broadcast_in_dim.137
  11.9 3.2 broadcast_select_fusion
  15.2 1.6 copy.18
  16.7 6.4 %all-to-all-start = ((bf16[2,16,256,128]{3,2,0,1:T(8,128)(2,1)}), bf16[2,16,256,128]{3,2,0,1:T(8,128)(2,1)S(1)}, u32[]{:S(2)}, u32[]{:S(2)}) async-start(bf16[2,16,256,128]{3,2,0,1:T(8,128)(2,1)} %copy.18), calls=%async_computation | async-start | bytes 4194304 | tf_op jit(solution)/shard_map/all_to_all | solution.py:111
  23.1 3.1 copy.19
  26.2 45.1 %all-to-all-done = bf16[2,16,256,128]{3,2,0,1:T(8,128)(2,1)S(1)} async-done(((bf16[2,16,256,128]{3,2,0,1:T(8,128)(2,1)}), bf16[2,16,256,128]{3,2,0,1:T(8,128)(2,1)S(1)}, u32[]{:S(2)}, u32[]{:S(2)}) %all-to-all-start) | async-done | bytes 2097184 | tf_op jit(solution)/shard_map/all_to_all | solution.py:111
  71.3 4.5 %all-to-all-start.1 = ((bf16[2,16,256,128]{3,2,0,1:T(8,128)(2,1)}), bf16[2,16,256,128]{3,2,0,1:T(8,128)(2,1)}, u32[]{:S(2)}, u32[]{:S(2)}) async-start(bf16[2,16,256,128]{3,2,0,1:T(8,128)(2,1)} %copy.19), calls=%async_computation.1 | async-start | bytes 4194304 | tf_op jit(solution)/shard_map/all_to_all | solution.py:112
  75.8 0.1 reshape.265
  75.9 2.6 gather_fusion.4
  78.5 2.0 collective-permute-start
  80.5 43.2 %all-to-all-done.1 = bf16[2,16,256,128]{3,2,0,1:T(8,128)(2,1)} async-done(((bf16[2,16,256,128]{3,2,0,1:T(8,128)(2,1)}), bf16[2,16,256,128]{3,2,0,1:T(8,128)(2,1)}, u32[]{:S(2)}, u32[]{:S(2)}) %all-to-all-start.1) | async-done | bytes 2097184 | tf_op jit(solution)/shard_map/all_to_all | solution.py:112
  123.7 3.7 %gather_fusion.6 = bf16[32,256,128]{2,1,0:T(8,128)(2,1)} fusion(bf16[2,16,256,128]{3,2,0,1:T(8,128)(2,1)} %all-to-all-done.1, s32[32]{0:T(128)S(1)} %reshape.265), kind=kCustom, calls=%fused_computation.6 | custom fusion | bytes 4194560 | tf_op jit(solution)/shard_map/vmap()/gather | solution.py:43
  127.4 3.9 %collective-permute-start.3 = (bf16[2,256,128]{2,1,0:T(8,128)(2,1)S(1)}, bf16[2,256,128]{2,1,0:T(8,128)(2,1)S(1)}, u32[]{:S(2)}, u32[]{:S(2)}) collective-permute-start(bf16[2,256,128]{2,1,0:T(8,128)(2,1)S(1)} %copy-done.5), channel_id=1, source_target_pairs={{0,4},{4,8},{8,12},{1,5},{5,9},{9,13},{2,6},{6,10},{10,14},{3,7},{... | collective-permute-start | bytes 393224 | tf_op jit(solution)/shard_map/ppermute | solution.py:14
  131.4 2.6 collective-permute-start.1
  134.0 24.2 %collective-permute-done = bf16[2,16,256,128]{3,2,1,0:T(8,128)(2,1)} collective-permute-done((bf16[2,16,256,128]{3,2,1,0:T(8,128)(2,1)S(1)}, bf16[2,16,256,128]{3,2,1,0:T(8,128)(2,1)}, u32[]{:S(2)}, u32[]{:S(2)}) %collective-permute-start) | collective-permute-done | bytes 2097184 | tf_op jit(solution)/shard_map/ppermute | solution.py:28
  158.2 43.1 %collective-permute-done.2 = bf16[2,16,256,128]{3,2,1,0:T(8,128)(2,1)} collective-permute-done((bf16[2,16,256,128]{3,2,1,0:T(8,128)(2,1)}, bf16[2,16,256,128]{3,2,1,0:T(8,128)(2,1)}, u32[]{:S(2)}, u32[]{:S(2)}) %collective-permute-start.2) | collective-permute-done | bytes 2097184 | tf_op jit(solution)/shard_map/ppermute | solution.py:28
  201.3 3.1 broadcast_select_fusion.3
  204.4 0.4 pad_maximum_fusion.3
  204.9 10.0 %pad_maximum_fusion.1 = bf16[2,8704,128]{2,1,0:T(8,128)(2,1)} fusion(bf16[2,256,128]{2,1,0:T(8,128)(2,1)S(1)} %copy-done.5, bf16[2,256,128]{2,1,0:T(8,128)(2,1)S(1)} %collective-permute-done.3, bf16[2,8192,128]{2,1,0:T(8,128)(2,1)S(1)} %bitcast.56), kind=kLoop, calls=%fused_computation.36 | loop fusion | flops 13369344 | bytes 8912896 | tf_op jit(solution)/shard_map/concatenate | solution.py:130
  214.9 0.4 pad_maximum_fusion.2
  215.3 9.9 %pad_maximum_fusion = bf16[2,8704,128]{2,1,0:T(8,128)(2,1)} fusion(bf16[2,256,128]{2,1,0:T(8,128)(2,1)S(1)} %copy-done.6, bf16[2,256,128]{2,1,0:T(8,128)(2,1)S(1)} %collective-permute-done.1, bf16[2,8192,128]{2,1,0:T(8,128)(2,1)S(1)} %bitcast.57), kind=kLoop, calls=%fused_computation.35 | loop fusion | flops 13369344 | bytes 8912896 | tf_op jit(solution)/shard_map/concatenate | solution.py:129
  225.2 136.7 %while.49 = (s32[]{:T(128)}, bf16[2,1024,128]{2,1,0:T(8,128)(2,1)S(1)}, bf16[2,1024,128]{2,1,0:T(8,128)(2,1)S(1)}, bf16[2,8704,128]{2,1,0:T(8,128)(2,1)}, bf16[2...) while((s32[]{:T(128)}, ...), condition=%wide.region_10.11_spmd.clone.clone, body=%wide.region_5.10_spmd.clone.clone.sunk | while | flops 2344288768 | bytes 68473648 | solution.py:157
  225.2 3.9 %dynamic-slice_bitcast_fusion.3 = (bf16[8704,128]{1,0:T(8,128)(2,1)}, bf16[8704,128]{1,0:T(8,128)(2,1)}) fusion(bf16[2,8704,128]{2,1,0:T(8,128)(2,1)} %get-tuple-element.681, s32[]{:T(128)} %get-tuple-element.668, bf16[2,8704,128]{2,1,0:T(8,128)(2,1)} %get-tuple-element.680), kind=kLoop, calls=%fused_computation.30.clone.1 | loop fusion | bytes 8912900 | tf_op jit(solution)/shard_map/while/body/jit(dynamic_index_in_dim)/squeeze | solution.py:157
  229.2 64.4 %while.50 = (s32[]{:T(128)}, bf16[2,512,128]{2,1,0:T(8,128)(2,1)S(1)}, s32[8704]{0:T(1024)S(1)}, s32[2]{0:T(128)S(1)}, pred[]{:T(512)}, /*index=5*/bf16[2,512,12...) while((s32[]{:T(128)}, ...), condition=%wide.region_9.9_spmd.clone, body=%wide.region_6.8_spmd.clone.sunk | while | flops 2344288768 | bytes 58477172 | solution.py:155
  229.2 0.6 dynamic_slice.85
  229.8 0.6 add_select_fusion.2
  230.4 13.1 %fusion.43 = (f32[512]{0:T(512)S(1)}, f32[512,8704]{1,0:T(8,128)}) fusion(bf16[8704,128]{1,0:T(8,128)(2,1)} %get-tuple-element.656, bf16[2,512,128]{2,1,0:T(8,128)(2,1)S(1)} %get-tuple-element.655, s32[]{:T(128)} %get-tuple-element.641, s32[8704]{0:T(1024)S(1)} %get-tuple-element.625, pred[8704]{0:T(1024)(128)(4,1)S(1)} %get-tuple-element.626, ...), kind=kOutput, calls=%fused_computation.75.clone.1 | convolution fusion | flops 1185414656 | bytes 20290564 | tf_op jit(solution)/shard_map/while/body/eval_jaxpr/while/body/eval_jaxpr/rd,kd->rk/dot_general | solution.py:51
  243.5 8.5 %fusion.44 = f32[512]{0:T(512)S(1)} fusion(f32[512,8704]{1,0:T(8,128)} %get-tuple-element.630, f32[512]{0:T(512)S(1)} %get-tuple-element.631), kind=kLoop, calls=%fused_computation.10.clone.1 | loop fusion | flops 8912384 | bytes 17829888 | tf_op jit(solution)/shard_map/while/body/eval_jaxpr/while/body/eval_jaxpr/reduce_sum | solution.py:58
  252.1 9.3 %fusion.45 = bf16[2,512,128]{2,1,0:T(8,128)(2,1)S(1)} fusion(bf16[2,512,128]{2,1,0:T(8,128)(2,1)S(1)} %get-tuple-element.642, s32[]{:T(128)} %get-tuple-element.641, bf16[8704,128]{1,0:T(8,128)(2,1)} %get-tuple-element.657, f32[512,8704]{1,0:T(8,128)} %get-tuple-element.630, f32[512]{0:T(512)S(1)} %get-tuple-element.631, f32[512]{0:T(512)S(1)} %fusion.44), kind=kOutput, calls=%fused_computation.17.clone.1 | convolution fusion | flops 1149894656 | bytes 20189188 | tf_op jit(solution)/shard_map/while/body/eval_jaxpr/while/body/eval_jaxpr/rk,kd->rd/dot_general | solution.py:59
  261.4 0.6 dynamic_slice.85
  262.0 0.6 add_select_fusion.2
  262.6 13.1 %fusion.43 = (f32[512]{0:T(512)S(1)}, f32[512,8704]{1,0:T(8,128)}) fusion(bf16[8704,128]{1,0:T(8,128)(2,1)} %get-tuple-element.656, bf16[2,512,128]{2,1,0:T(8,128)(2,1)S(1)} %get-tuple-element.655, s32[]{:T(128)} %get-tuple-element.641, s32[8704]{0:T(1024)S(1)} %get-tuple-element.625, pred[8704]{0:T(1024)(128)(4,1)S(1)} %get-tuple-element.626, ...), kind=kOutput, calls=%fused_computation.75.clone.1 | convolution fusion | flops 1185414656 | bytes 20290564 | tf_op jit(solution)/shard_map/while/body/eval_jaxpr/while/body/eval_jaxpr/rd,kd->rk/dot_general | solution.py:51
  275.7 8.5 %fusion.44 = f32[512]{0:T(512)S(1)} fusion(f32[512,8704]{1,0:T(8,128)} %get-tuple-element.630, f32[512]{0:T(512)S(1)} %get-tuple-element.631), kind=kLoop, calls=%fused_computation.10.clone.1 | loop fusion | flops 8912384 | bytes 17829888 | tf_op jit(solution)/shard_map/while/body/eval_jaxpr/while/body/eval_jaxpr/reduce_sum | solution.py:58
  284.2 9.3 %fusion.45 = bf16[2,512,128]{2,1,0:T(8,128)(2,1)S(1)} fusion(bf16[2,512,128]{2,1,0:T(8,128)(2,1)S(1)} %get-tuple-element.642, s32[]{:T(128)} %get-tuple-element.641, bf16[8704,128]{1,0:T(8,128)(2,1)} %get-tuple-element.657, f32[512,8704]{1,0:T(8,128)} %get-tuple-element.630, f32[512]{0:T(512)S(1)} %get-tuple-element.631, f32[512]{0:T(512)S(1)} %fusion.44), kind=kOutput, calls=%fused_computation.17.clone.1 | convolution fusion | flops 1149894656 | bytes 20189188 | tf_op jit(solution)/shard_map/while/body/eval_jaxpr/while/body/eval_jaxpr/rk,kd->rd/dot_general | solution.py:59
  293.6 3.9 %dynamic-slice_bitcast_fusion.3 = (bf16[8704,128]{1,0:T(8,128)(2,1)}, bf16[8704,128]{1,0:T(8,128)(2,1)}) fusion(bf16[2,8704,128]{2,1,0:T(8,128)(2,1)} %get-tuple-element.681, s32[]{:T(128)} %get-tuple-element.668, bf16[2,8704,128]{2,1,0:T(8,128)(2,1)} %get-tuple-element.680), kind=kLoop, calls=%fused_computation.30.clone.1 | loop fusion | bytes 8912900 | tf_op jit(solution)/shard_map/while/body/jit(dynamic_index_in_dim)/squeeze | solution.py:157
  297.5 64.4 %while.50 = (s32[]{:T(128)}, bf16[2,512,128]{2,1,0:T(8,128)(2,1)S(1)}, s32[8704]{0:T(1024)S(1)}, s32[2]{0:T(128)S(1)}, pred[]{:T(512)}, /*index=5*/bf16[2,512,12...) while((s32[]{:T(128)}, ...), condition=%wide.region_9.9_spmd.clone, body=%wide.region_6.8_spmd.clone.sunk | while | flops 2344288768 | bytes 58477172 | solution.py:155
  297.6 0.6 dynamic_slice.85
  298.2 0.6 add_select_fusion.2
  298.8 13.1 %fusion.43 = (f32[512]{0:T(512)S(1)}, f32[512,8704]{1,0:T(8,128)}) fusion(bf16[8704,128]{1,0:T(8,128)(2,1)} %get-tuple-element.656, bf16[2,512,128]{2,1,0:T(8,128)(2,1)S(1)} %get-tuple-element.655, s32[]{:T(128)} %get-tuple-element.641, s32[8704]{0:T(1024)S(1)} %get-tuple-element.625, pred[8704]{0:T(1024)(128)(4,1)S(1)} %get-tuple-element.626, ...), kind=kOutput, calls=%fused_computation.75.clone.1 | convolution fusion | flops 1185414656 | bytes 20290564 | tf_op jit(solution)/shard_map/while/body/eval_jaxpr/while/body/eval_jaxpr/rd,kd->rk/dot_general | solution.py:51
  311.9 8.5 %fusion.44 = f32[512]{0:T(512)S(1)} fusion(f32[512,8704]{1,0:T(8,128)} %get-tuple-element.630, f32[512]{0:T(512)S(1)} %get-tuple-element.631), kind=kLoop, calls=%fused_computation.10.clone.1 | loop fusion | flops 8912384 | bytes 17829888 | tf_op jit(solution)/shard_map/while/body/eval_jaxpr/while/body/eval_jaxpr/reduce_sum | solution.py:58
  320.4 9.3 %fusion.45 = bf16[2,512,128]{2,1,0:T(8,128)(2,1)S(1)} fusion(bf16[2,512,128]{2,1,0:T(8,128)(2,1)S(1)} %get-tuple-element.642, s32[]{:T(128)} %get-tuple-element.641, bf16[8704,128]{1,0:T(8,128)(2,1)} %get-tuple-element.657, f32[512,8704]{1,0:T(8,128)} %get-tuple-element.630, f32[512]{0:T(512)S(1)} %get-tuple-element.631, f32[512]{0:T(512)S(1)} %fusion.44), kind=kOutput, calls=%fused_computation.17.clone.1 | convolution fusion | flops 1149894656 | bytes 20189188 | tf_op jit(solution)/shard_map/while/body/eval_jaxpr/while/body/eval_jaxpr/rk,kd->rd/dot_general | solution.py:59
  329.8 0.6 dynamic_slice.85
  330.4 0.6 add_select_fusion.2
  331.0 13.1 %fusion.43 = (f32[512]{0:T(512)S(1)}, f32[512,8704]{1,0:T(8,128)}) fusion(bf16[8704,128]{1,0:T(8,128)(2,1)} %get-tuple-element.656, bf16[2,512,128]{2,1,0:T(8,128)(2,1)S(1)} %get-tuple-element.655, s32[]{:T(128)} %get-tuple-element.641, s32[8704]{0:T(1024)S(1)} %get-tuple-element.625, pred[8704]{0:T(1024)(128)(4,1)S(1)} %get-tuple-element.626, ...), kind=kOutput, calls=%fused_computation.75.clone.1 | convolution fusion | flops 1185414656 | bytes 20290564 | tf_op jit(solution)/shard_map/while/body/eval_jaxpr/while/body/eval_jaxpr/rd,kd->rk/dot_general | solution.py:51
  344.1 8.5 %fusion.44 = f32[512]{0:T(512)S(1)} fusion(f32[512,8704]{1,0:T(8,128)} %get-tuple-element.630, f32[512]{0:T(512)S(1)} %get-tuple-element.631), kind=kLoop, calls=%fused_computation.10.clone.1 | loop fusion | flops 8912384 | bytes 17829888 | tf_op jit(solution)/shard_map/while/body/eval_jaxpr/while/body/eval_jaxpr/reduce_sum | solution.py:58
  352.6 9.3 %fusion.45 = bf16[2,512,128]{2,1,0:T(8,128)(2,1)S(1)} fusion(bf16[2,512,128]{2,1,0:T(8,128)(2,1)S(1)} %get-tuple-element.642, s32[]{:T(128)} %get-tuple-element.641, bf16[8704,128]{1,0:T(8,128)(2,1)} %get-tuple-element.657, f32[512,8704]{1,0:T(8,128)} %get-tuple-element.630, f32[512]{0:T(512)S(1)} %get-tuple-element.631, f32[512]{0:T(512)S(1)} %fusion.44), kind=kOutput, calls=%fused_computation.17.clone.1 | convolution fusion | flops 1149894656 | bytes 20189188 | tf_op jit(solution)/shard_map/while/body/eval_jaxpr/while/body/eval_jaxpr/rk,kd->rd/dot_general | solution.py:59
  362.0 0.0 copy-start.7
  362.0 0.8 copy-done.7
  362.8 1.0 copy-done.1
  (43 shorter events, 0.4 us)
Async XLA Ops:
  0.0 5.8 %copy-start = (bf16[2,4096,128]{2,1,0:T(8,128)(2,1)S(1)}, bf16[2,4096,128]{2,1,0:T(8,128)(2,1)}, u32[]{:S(2)}) copy-start(bf16[2,4096,128]{2,1,0:T(8,128)(2,1)} %param.19) | copy-start | bytes 6291460
  7.9 4.0 %copy-start.3 = (bf16[32,256,128]{2,1,0:T(8,128)(2,1)S(1)}, bf16[32,256,128]{2,1,0:T(8,128)(2,1)}, u32[]{:S(2)}) copy-start(bf16[32,256,128]{2,1,0:T(8,128)(2,1)} %gather_fusion.3) | copy-start | bytes 6291460
  16.7 54.6 %all-to-all-start = ((bf16[2,16,256,128]{3,2,0,1:T(8,128)(2,1)}), bf16[2,16,256,128]{3,2,0,1:T(8,128)(2,1)S(1)}, u32[]{:S(2)}, u32[]{:S(2)}) async-start(bf16[2,16,256,128]{3,2,0,1:T(8,128)(2,1)} %copy.18), calls=%async_computation | async-start | bytes 4194304 | tf_op jit(solution)/shard_map/all_to_all | solution.py:111
  71.3 4.5 %copy-start.2 = (bf16[2,16,256,128]{3,2,0,1:T(8,128)(2,1)}, bf16[2,16,256,128]{3,2,0,1:T(8,128)(2,1)S(1)}, u32[]{:S(2)}) copy-start(bf16[2,16,256,128]{3,2,0,1:T(8,128)(2,1)S(1)} %all-to-all-done) | copy-start | bytes 6291460
  71.3 52.4 %all-to-all-start.1 = ((bf16[2,16,256,128]{3,2,0,1:T(8,128)(2,1)}), bf16[2,16,256,128]{3,2,0,1:T(8,128)(2,1)}, u32[]{:S(2)}, u32[]{:S(2)}) async-start(bf16[2,16,256,128]{3,2,0,1:T(8,128)(2,1)} %copy.19), calls=%async_computation.1 | async-start | bytes 4194304 | tf_op jit(solution)/shard_map/all_to_all | solution.py:112
  75.9 51.5 %copy-start.5 = (bf16[2,256,128]{2,1,0:T(8,128)(2,1)S(1)}, bf16[2,256,128]{2,1,0:T(8,128)(2,1)}, u32[]{:S(2)}) copy-start(bf16[2,256,128]{2,1,0:T(8,128)(2,1)} %param.18) | copy-start | bytes 393220
  75.9 55.5 %copy-start.6 = (bf16[2,256,128]{2,1,0:T(8,128)(2,1)S(1)}, bf16[2,256,128]{2,1,0:T(8,128)(2,1)}, u32[]{:S(2)}) copy-start(bf16[2,256,128]{2,1,0:T(8,128)(2,1)} %param.17) | copy-start | bytes 393220
  78.5 79.7 %collective-permute-start = (bf16[2,16,256,128]{3,2,1,0:T(8,128)(2,1)S(1)}, bf16[2,16,256,128]{3,2,1,0:T(8,128)(2,1)}, u32[]{:S(2)}, u32[]{:S(2)}) collective-permute-start(bf16[2,16,256,128]{3,2,1,0:T(8,128)(2,1)S(1)} %bitcast.58), channel_id=1, source_target_pairs={{0,4},{4,0},{8,12},{12,8},{1,5},{5,1},{9,13},{13,9},{2,6},{6,2},{1... | collective-permute-start | bytes 6291464 | tf_op jit(solution)/shard_map/ppermute | solution.py:28
  127.4 73.9 %collective-permute-start.2 = (bf16[2,16,256,128]{3,2,1,0:T(8,128)(2,1)}, bf16[2,16,256,128]{3,2,1,0:T(8,128)(2,1)}, u32[]{:S(2)}, u32[]{:S(2)}) collective-permute-start(bf16[2,16,256,128]{3,2,1,0:T(8,128)(2,1)} %bitcast.60), channel_id=1, source_target_pairs={{0,4},{4,0},{8,12},{12,8},{1,5},{5,1},{9,13},{13,9},{2,6},{6,2},{1... | collective-permute-start | bytes 6291464 | tf_op jit(solution)/shard_map/ppermute | solution.py:28
  127.4 77.5 %collective-permute-start.3 = (bf16[2,256,128]{2,1,0:T(8,128)(2,1)S(1)}, bf16[2,256,128]{2,1,0:T(8,128)(2,1)S(1)}, u32[]{:S(2)}, u32[]{:S(2)}) collective-permute-start(bf16[2,256,128]{2,1,0:T(8,128)(2,1)S(1)} %copy-done.5), channel_id=1, source_target_pairs={{0,4},{4,8},{8,12},{1,5},{5,9},{9,13},{2,6},{6,10},{10,14},{3,7},{... | collective-permute-start | bytes 393224 | tf_op jit(solution)/shard_map/ppermute | solution.py:14
  131.4 83.9 %collective-permute-start.1 = (bf16[2,256,128]{2,1,0:T(8,128)(2,1)S(1)}, bf16[2,256,128]{2,1,0:T(8,128)(2,1)S(1)}, u32[]{:S(2)}, u32[]{:S(2)}) collective-permute-start(bf16[2,256,128]{2,1,0:T(8,128)(2,1)S(1)} %copy-done.6), channel_id=1, source_target_pairs={{0,4},{4,8},{8,12},{1,5},{5,9},{9,13},{2,6},{6,10},{10,14},{3,7},{... | collective-permute-start | bytes 393224 | tf_op jit(solution)/shard_map/ppermute | solution.py:14
  215.3 9.9 %copy-start.4 = (bf16[8,256,128]{2,1,0:T(8,128)(2,1)S(1)}, bf16[8,256,128]{2,1,0:T(8,128)(2,1)}, u32[]{:S(2)}) copy-start(bf16[8,256,128]{2,1,0:T(8,128)(2,1)} %param.16) | copy-start | bytes 1572868
  362.0 0.8 copy-start.7
  362.0 1.8 copy-start.1
where the time goes:
time: 365 us; the launch traced here: 364 us
  waiting for transfers between devices  156 us (43%)
  matrix products  89.4 us (24%)
  other arithmetic  67.8 us (19%)
  local copies, waits for them, and re-layouts  31.2 us (9%)
  starting transfers between devices  19.4 us (5%)
    ppermute x2, waiting for transfers between devices, partner(): return lax.ppermute(value, axis, pairs)  67.3 us
    dot_general x4, matrix products, attend(): jnp.einsum('rd,kd->rk', query_rows, all_keys, preferred_element_type=jnp....  52.3 us
    all_to_all x1, waiting for transfers between devices, shards(): lax.all_to_all(sent_keys, 'ctx', split_axis=1, concat_axis=1, tiled=True)  45.1 us
    all_to_all x1, waiting for transfers between devices, shards(): lax.all_to_all(sent_values, 'ctx', split_axis=1, concat_axis=1, tiled=True)  43.2 us
    dot_general x4, matrix products, attend(): jnp.einsum('rk,kd->rd', weights.astype(jnp.bfloat16), all_values, preferr...  37.1 us
    reduce_sum x4, other arithmetic, attend(): weight_sum = jnp.sum(weights, axis=-1, keepdims=True)  34.2 us
    gather x6, local copies, waits for them, and re-layouts, pick_rows(): return source[indices]  12.5 us
    concatenate x1, other arithmetic, shards(): jnp.concatenate([live_values, prev_values, stretch_values], axis=1)  9.97 us
  transfers between devices with their start and end apart: 6, of which 4 were waited for; matrix products, arithmetic and copies ran while one was open for 6% of the time, Pallas kernels for 0%

commit v1 on v0

--- a/solution.py
+++ b/solution.py
@@ -107,8 +107,17 @@
     sent_values = jnp.where(
         usable[:, :, None, None], take_blocks(value_halves, half_index), 0
     ).astype(jnp.bfloat16)
+    orders_carry = lambda here_x: jnp.concatenate(
+        jax.lax.all_to_all(
+            jnp.stack(jnp.split(here_x, jax.lax.axis_size("ctx"), axis=1)),
+            axis_name="ctx",
+            split_axis=0,
+            concat_axis=0,
+        ),
+        axis=1,
+    )
     got_keys, got_values = (
-        lax.all_to_all(sent_keys, "ctx", split_axis=1, concat_axis=1, tiled=True),
+        orders_carry(sent_keys),
         lax.all_to_all(sent_values, "ctx", split_axis=1, concat_axis=1, tiled=True),
     )
     mine_keys = take_blocks(got_keys, my_slot)

time: 365 us -> 365 us (level)
  transfers between devices with their start and end apart: 6 -> 6, of which waited for: 4 -> 4; matrix products, arithmetic and copies ran while one was open for 6% -> 7% of each run, Pallas kernels for 0% -> 0%
where the time goes in v1:
time: 365 us; the launch traced here: 364 us
  waiting for transfers between devices  154 us (42%)
  matrix products  89.4 us (24%)
  other arithmetic  70 us (19%)
  local copies, waits for them, and re-layouts  31.2 us (9%)
  starting transfers between devices  19.4 us (5%)
    ppermute x2, waiting for transfers between devices, partner(): return lax.ppermute(value, axis, pairs)  67.3 us
    dot_general x4, matrix products, attend(): jnp.einsum('rd,kd->rk', query_rows, all_keys, preferred_element_type=jnp....  52.3 us
    all_to_all x1, waiting for transfers between devices, shards(): jax.lax.all_to_all(jnp.stack(jnp.split(here_x, jax.lax.axis_size('ctx'),...  45 us
    all_to_all x1, waiting for transfers between devices, shards(): lax.all_to_all(sent_values, 'ctx', split_axis=1, concat_axis=1, tiled=True)  41.7 us
    dot_general x4, matrix products, attend(): jnp.einsum('rk,kd->rd', weights.astype(jnp.bfloat16), all_values, preferr...  37.1 us
    reduce_sum x4, other arithmetic, attend(): weight_sum = jnp.sum(weights, axis=-1, keepdims=True)  34.2 us
    gather x6, local copies, waits for them, and re-layouts, pick_rows(): return source[indices]  12.3 us
    concatenate x1, other arithmetic, shards(): jnp.concatenate([live_values, prev_values, stretch_values], axis=1)  9.97 us
  transfers between devices with their start and end apart: 6, of which 4 were waited for; matrix products, arithmetic and copies ran while one was open for 7% of the time, Pallas kernels for 0%

profile of v1, /device:TPU:0, one launch (start us, length us, event | category | flops | bytes accessed | tf_op | source)
XLA Modules:
  0.0 364.5 jit_solution(1419883446588091762)
XLA Ops:
  0.1 0.9 select_reduce_fusion.2
  1.0 0.9 select_reduce_fusion
  1.9 0.7 pad_clamp_fusion
  2.6 0.6 gather_fusion
  3.1 0.2 convert_reduce_fusion
  3.4 0.6 gather_fusion.1
  3.9 0.6 gather_fusion.2
  4.5 0.2 fusion.24
  4.7 0.2 select_reduce_fusion.1
  5.0 0.1 mul.65
  5.1 0.7 fusion.27
  5.7 0.1 reshape.267
  5.8 2.1 gather_fusion.5
  8.0 3.7 %gather_fusion.3 = bf16[32,256,128]{2,1,0:T(8,128)(2,1)} fusion(bf16[2,16,256,128]{3,2,1,0:T(8,128)(2,1)} %bitcast.79, s32[32]{0:T(128)S(1)} %reshape.267), kind=kCustom, calls=%fused_computation.3 | custom fusion | bytes 4194560 | tf_op jit(solution)/shard_map/vmap()/gather | solution.py:43
  11.7 0.1 broadcast_in_dim.137
  11.8 3.9 %broadcast_select_fusion = (bf16[2,16,256,128]{3,2,1,0:T(8,128)(2,1)}, bf16[2,16,256,128]{3,2,1,0:T(8,128)(2,1)S(1)}) fusion(bf16[2,16,256,128]{3,2,1,0:T(8,128)(2,1)} %bitcast.74, pred[2,16]{1,0:T(4,128)(4,1)S(1)} %broadcast_in_dim.137, bf16[2,16,256,128]{3,2,1,0:T(8,128)(2,1)} %bitcast.75), kind=kLoop, calls=%fused_computation.40 | loop fusion | flops 2097152 | bytes 8388640 | tf_op jit(solution)/shard_map/jit(_where)/select_n | solution.py:107
  15.7 0.1 slice_bitcast_fusion.3
  15.8 1.6 pad_maximum_fusion.4
  17.4 6.4 %all-to-all-start = ((bf16[4,2,4,256,128]{4,3,2,1,0:T(8,128)(2,1)}), bf16[4,2,4,256,128]{4,3,2,1,0:T(8,128)(2,1)S(1)}, u32[]{:S(2)}, u32[]{:S(2)}) async-start(bf16[4,2,4,256,128]{4,3,2,1,0:T(8,128)(2,1)} %pad_maximum_fusion.4), calls=%async_computation | async-start | bytes 4194304 | tf_op jit(solution)/shard_map/all_to_all | solution.py:111
  23.7 3.1 copy.21
  26.9 45.0 %all-to-all-done = bf16[4,2,4,256,128]{4,3,2,1,0:T(8,128)(2,1)S(1)} async-done(((bf16[4,2,4,256,128]{4,3,2,1,0:T(8,128)(2,1)}), bf16[4,2,4,256,128]{4,3,2,1,0:T(8,128)(2,1)S(1)}, u32[]{:S(2)}, u32[]{:S(2)}) %all-to-all-start) | async-done | bytes 2097184 | tf_op jit(solution)/shard_map/all_to_all | solution.py:111
  71.9 4.4 %all-to-all-start.1 = ((bf16[2,16,256,128]{3,2,0,1:T(8,128)(2,1)}), bf16[2,16,256,128]{3,2,0,1:T(8,128)(2,1)}, u32[]{:S(2)}, u32[]{:S(2)}) async-start(bf16[2,16,256,128]{3,2,0,1:T(8,128)(2,1)} %copy.21), calls=%async_computation.1 | async-start | bytes 4194304 | tf_op jit(solution)/shard_map/all_to_all | solution.py:121
  76.4 0.1 reshape.273
  76.5 1.5 copy.20
  78.0 2.5 gather_fusion.4
  80.6 2.0 collective-permute-start
  82.6 41.7 %all-to-all-done.1 = bf16[2,16,256,128]{3,2,0,1:T(8,128)(2,1)} async-done(((bf16[2,16,256,128]{3,2,0,1:T(8,128)(2,1)}), bf16[2,16,256,128]{3,2,0,1:T(8,128)(2,1)}, u32[]{:S(2)}, u32[]{:S(2)}) %all-to-all-start.1) | async-done | bytes 2097184 | tf_op jit(solution)/shard_map/all_to_all | solution.py:121
  124.3 3.7 %gather_fusion.6 = bf16[32,256,128]{2,1,0:T(8,128)(2,1)} fusion(bf16[2,16,256,128]{3,2,0,1:T(8,128)(2,1)} %all-to-all-done.1, s32[32]{0:T(128)S(1)} %reshape.273), kind=kCustom, calls=%fused_computation.6 | custom fusion | bytes 4194560 | tf_op jit(solution)/shard_map/vmap()/gather | solution.py:43
  128.1 3.9 %collective-permute-start.3 = (bf16[2,256,128]{2,1,0:T(8,128)(2,1)S(1)}, bf16[2,256,128]{2,1,0:T(8,128)(2,1)S(1)}, u32[]{:S(2)}, u32[]{:S(2)}) collective-permute-start(bf16[2,256,128]{2,1,0:T(8,128)(2,1)S(1)} %copy-done.3), channel_id=1, source_target_pairs={{0,4},{4,8},{8,12},{1,5},{5,9},{9,13},{2,6},{6,10},{10,14},{3,7},{... | collective-permute-start | bytes 393224 | tf_op jit(solution)/shard_map/ppermute | solution.py:14
  132.0 2.6 collective-permute-start.1
  134.7 24.2 %collective-permute-done = bf16[2,16,256,128]{3,2,1,0:T(8,128)(2,1)} collective-permute-done((bf16[2,16,256,128]{3,2,1,0:T(8,128)(2,1)S(1)}, bf16[2,16,256,128]{3,2,1,0:T(8,128)(2,1)}, u32[]{:S(2)}, u32[]{:S(2)}) %collective-permute-start) | collective-permute-done | bytes 2097184 | tf_op jit(solution)/shard_map/ppermute | solution.py:28
  158.8 43.1 %collective-permute-done.2 = bf16[2,16,256,128]{3,2,1,0:T(8,128)(2,1)} collective-permute-done((bf16[2,16,256,128]{3,2,1,0:T(8,128)(2,1)}, bf16[2,16,256,128]{3,2,1,0:T(8,128)(2,1)}, u32[]{:S(2)}, u32[]{:S(2)}) %collective-permute-start.2) | collective-permute-done | bytes 2097184 | tf_op jit(solution)/shard_map/ppermute | solution.py:28
  202.0 3.1 broadcast_select_fusion.3
  205.1 0.4 pad_maximum_fusion.3
  205.5 10.0 %pad_maximum_fusion.1 = bf16[2,8704,128]{2,1,0:T(8,128)(2,1)} fusion(bf16[2,256,128]{2,1,0:T(8,128)(2,1)S(1)} %copy-done.3, bf16[2,256,128]{2,1,0:T(8,128)(2,1)S(1)} %collective-permute-done.3, bf16[2,8192,128]{2,1,0:T(8,128)(2,1)S(1)} %bitcast.67), kind=kLoop, calls=%fused_computation.36 | loop fusion | flops 13369344 | bytes 8912896 | tf_op jit(solution)/shard_map/concatenate | solution.py:139
  215.5 0.4 pad_maximum_fusion.2
  216.0 9.9 %pad_maximum_fusion = bf16[2,8704,128]{2,1,0:T(8,128)(2,1)} fusion(bf16[2,256,128]{2,1,0:T(8,128)(2,1)S(1)} %copy-done.4, bf16[2,256,128]{2,1,0:T(8,128)(2,1)S(1)} %collective-permute-done.1, bf16[2,8192,128]{2,1,0:T(8,128)(2,1)S(1)} %bitcast.68), kind=kLoop, calls=%fused_computation.35 | loop fusion | flops 13369344 | bytes 8912896 | tf_op jit(solution)/shard_map/concatenate | solution.py:138
  225.8 136.8 %while.49 = (s32[]{:T(128)}, bf16[2,1024,128]{2,1,0:T(8,128)(2,1)S(1)}, bf16[2,1024,128]{2,1,0:T(8,128)(2,1)S(1)}, bf16[2,8704,128]{2,1,0:T(8,128)(2,1)}, bf16[2...) while((s32[]{:T(128)}, ...), condition=%wide.region_10.11_spmd.clone.clone, body=%wide.region_5.10_spmd.clone.clone.sunk | while | flops 2344288768 | bytes 68473648 | solution.py:166
  225.8 3.9 %dynamic-slice_bitcast_fusion.3 = (bf16[8704,128]{1,0:T(8,128)(2,1)}, bf16[8704,128]{1,0:T(8,128)(2,1)}) fusion(bf16[2,8704,128]{2,1,0:T(8,128)(2,1)} %get-tuple-element.685, s32[]{:T(128)} %get-tuple-element.672, bf16[2,8704,128]{2,1,0:T(8,128)(2,1)} %get-tuple-element.684), kind=kLoop, calls=%fused_computation.30.clone.1 | loop fusion | bytes 8912900 | tf_op jit(solution)/shard_map/while/body/jit(dynamic_index_in_dim)/squeeze | solution.py:166
  229.8 64.4 %while.50 = (s32[]{:T(128)}, bf16[2,512,128]{2,1,0:T(8,128)(2,1)S(1)}, s32[8704]{0:T(1024)S(1)}, s32[2]{0:T(128)S(1)}, pred[]{:T(512)}, /*index=5*/bf16[2,512,12...) while((s32[]{:T(128)}, ...), condition=%wide.region_9.9_spmd.clone, body=%wide.region_6.8_spmd.clone.sunk | while | flops 2344288768 | bytes 58477172 | solution.py:164
  229.8 0.6 dynamic_slice.85
  230.5 0.6 add_select_fusion.2
  231.1 13.1 %fusion.43 = (f32[512]{0:T(512)S(1)}, f32[512,8704]{1,0:T(8,128)}) fusion(bf16[8704,128]{1,0:T(8,128)(2,1)} %get-tuple-element.660, bf16[2,512,128]{2,1,0:T(8,128)(2,1)S(1)} %get-tuple-element.659, s32[]{:T(128)} %get-tuple-element.645, s32[8704]{0:T(1024)S(1)} %get-tuple-element.629, pred[8704]{0:T(1024)(128)(4,1)S(1)} %get-tuple-element.630, ...), kind=kOutput, calls=%fused_computation.80.clone.1 | convolution fusion | flops 1185414656 | bytes 20290564 | tf_op jit(solution)/shard_map/while/body/eval_jaxpr/while/body/eval_jaxpr/rd,kd->rk/dot_general | solution.py:51
  244.2 8.5 %fusion.44 = f32[512]{0:T(512)S(1)} fusion(f32[512,8704]{1,0:T(8,128)} %get-tuple-element.634, f32[512]{0:T(512)S(1)} %get-tuple-element.635), kind=kLoop, calls=%fused_computation.10.clone.1 | loop fusion | flops 8912384 | bytes 17829888 | tf_op jit(solution)/shard_map/while/body/eval_jaxpr/while/body/eval_jaxpr/reduce_sum | solution.py:58
  252.7 9.3 %fusion.45 = bf16[2,512,128]{2,1,0:T(8,128)(2,1)S(1)} fusion(bf16[2,512,128]{2,1,0:T(8,128)(2,1)S(1)} %get-tuple-element.646, s32[]{:T(128)} %get-tuple-element.645, bf16[8704,128]{1,0:T(8,128)(2,1)} %get-tuple-element.661, f32[512,8704]{1,0:T(8,128)} %get-tuple-element.634, f32[512]{0:T(512)S(1)} %get-tuple-element.635, f32[512]{0:T(512)S(1)} %fusion.44), kind=kOutput, calls=%fused_computation.17.clone.1 | convolution fusion | flops 1149894656 | bytes 20189188 | tf_op jit(solution)/shard_map/while/body/eval_jaxpr/while/body/eval_jaxpr/rk,kd->rd/dot_general | solution.py:59
  262.0 0.6 dynamic_slice.85
  262.7 0.6 add_select_fusion.2
  263.3 13.1 %fusion.43 = (f32[512]{0:T(512)S(1)}, f32[512,8704]{1,0:T(8,128)}) fusion(bf16[8704,128]{1,0:T(8,128)(2,1)} %get-tuple-element.660, bf16[2,512,128]{2,1,0:T(8,128)(2,1)S(1)} %get-tuple-element.659, s32[]{:T(128)} %get-tuple-element.645, s32[8704]{0:T(1024)S(1)} %get-tuple-element.629, pred[8704]{0:T(1024)(128)(4,1)S(1)} %get-tuple-element.630, ...), kind=kOutput, calls=%fused_computation.80.clone.1 | convolution fusion | flops 1185414656 | bytes 20290564 | tf_op jit(solution)/shard_map/while/body/eval_jaxpr/while/body/eval_jaxpr/rd,kd->rk/dot_general | solution.py:51
  276.4 8.5 %fusion.44 = f32[512]{0:T(512)S(1)} fusion(f32[512,8704]{1,0:T(8,128)} %get-tuple-element.634, f32[512]{0:T(512)S(1)} %get-tuple-element.635), kind=kLoop, calls=%fused_computation.10.clone.1 | loop fusion | flops 8912384 | bytes 17829888 | tf_op jit(solution)/shard_map/while/body/eval_jaxpr/while/body/eval_jaxpr/reduce_sum | solution.py:58
  284.9 9.3 %fusion.45 = bf16[2,512,128]{2,1,0:T(8,128)(2,1)S(1)} fusion(bf16[2,512,128]{2,1,0:T(8,128)(2,1)S(1)} %get-tuple-element.646, s32[]{:T(128)} %get-tuple-element.645, bf16[8704,128]{1,0:T(8,128)(2,1)} %get-tuple-element.661, f32[512,8704]{1,0:T(8,128)} %get-tuple-element.634, f32[512]{0:T(512)S(1)} %get-tuple-element.635, f32[512]{0:T(512)S(1)} %fusion.44), kind=kOutput, calls=%fused_computation.17.clone.1 | convolution fusion | flops 1149894656 | bytes 20189188 | tf_op jit(solution)/shard_map/while/body/eval_jaxpr/while/body/eval_jaxpr/rk,kd->rd/dot_general | solution.py:59
  294.3 3.9 %dynamic-slice_bitcast_fusion.3 = (bf16[8704,128]{1,0:T(8,128)(2,1)}, bf16[8704,128]{1,0:T(8,128)(2,1)}) fusion(bf16[2,8704,128]{2,1,0:T(8,128)(2,1)} %get-tuple-element.685, s32[]{:T(128)} %get-tuple-element.672, bf16[2,8704,128]{2,1,0:T(8,128)(2,1)} %get-tuple-element.684), kind=kLoop, calls=%fused_computation.30.clone.1 | loop fusion | bytes 8912900 | tf_op jit(solution)/shard_map/while/body/jit(dynamic_index_in_dim)/squeeze | solution.py:166
  298.2 64.4 %while.50 = (s32[]{:T(128)}, bf16[2,512,128]{2,1,0:T(8,128)(2,1)S(1)}, s32[8704]{0:T(1024)S(1)}, s32[2]{0:T(128)S(1)}, pred[]{:T(512)}, /*index=5*/bf16[2,512,12...) while((s32[]{:T(128)}, ...), condition=%wide.region_9.9_spmd.clone, body=%wide.region_6.8_spmd.clone.sunk | while | flops 2344288768 | bytes 58477172 | solution.py:164
  298.3 0.6 dynamic_slice.85
  298.9 0.6 add_select_fusion.2
  299.5 13.1 %fusion.43 = (f32[512]{0:T(512)S(1)}, f32[512,8704]{1,0:T(8,128)}) fusion(bf16[8704,128]{1,0:T(8,128)(2,1)} %get-tuple-element.660, bf16[2,512,128]{2,1,0:T(8,128)(2,1)S(1)} %get-tuple-element.659, s32[]{:T(128)} %get-tuple-element.645, s32[8704]{0:T(1024)S(1)} %get-tuple-element.629, pred[8704]{0:T(1024)(128)(4,1)S(1)} %get-tuple-element.630, ...), kind=kOutput, calls=%fused_computation.80.clone.1 | convolution fusion | flops 1185414656 | bytes 20290564 | tf_op jit(solution)/shard_map/while/body/eval_jaxpr/while/body/eval_jaxpr/rd,kd->rk/dot_general | solution.py:51
  312.6 8.5 %fusion.44 = f32[512]{0:T(512)S(1)} fusion(f32[512,8704]{1,0:T(8,128)} %get-tuple-element.634, f32[512]{0:T(512)S(1)} %get-tuple-element.635), kind=kLoop, calls=%fused_computation.10.clone.1 | loop fusion | flops 8912384 | bytes 17829888 | tf_op jit(solution)/shard_map/while/body/eval_jaxpr/while/body/eval_jaxpr/reduce_sum | solution.py:58
  321.1 9.3 %fusion.45 = bf16[2,512,128]{2,1,0:T(8,128)(2,1)S(1)} fusion(bf16[2,512,128]{2,1,0:T(8,128)(2,1)S(1)} %get-tuple-element.646, s32[]{:T(128)} %get-tuple-element.645, bf16[8704,128]{1,0:T(8,128)(2,1)} %get-tuple-element.661, f32[512,8704]{1,0:T(8,128)} %get-tuple-element.634, f32[512]{0:T(512)S(1)} %get-tuple-element.635, f32[512]{0:T(512)S(1)} %fusion.44), kind=kOutput, calls=%fused_computation.17.clone.1 | convolution fusion | flops 1149894656 | bytes 20189188 | tf_op jit(solution)/shard_map/while/body/eval_jaxpr/while/body/eval_jaxpr/rk,kd->rd/dot_general | solution.py:59
  330.5 0.6 dynamic_slice.85
  331.1 0.6 add_select_fusion.2
  331.7 13.1 %fusion.43 = (f32[512]{0:T(512)S(1)}, f32[512,8704]{1,0:T(8,128)}) fusion(bf16[8704,128]{1,0:T(8,128)(2,1)} %get-tuple-element.660, bf16[2,512,128]{2,1,0:T(8,128)(2,1)S(1)} %get-tuple-element.659, s32[]{:T(128)} %get-tuple-element.645, s32[8704]{0:T(1024)S(1)} %get-tuple-element.629, pred[8704]{0:T(1024)(128)(4,1)S(1)} %get-tuple-element.630, ...), kind=kOutput, calls=%fused_computation.80.clone.1 | convolution fusion | flops 1185414656 | bytes 20290564 | tf_op jit(solution)/shard_map/while/body/eval_jaxpr/while/body/eval_jaxpr/rd,kd->rk/dot_general | solution.py:51
  344.8 8.5 %fusion.44 = f32[512]{0:T(512)S(1)} fusion(f32[512,8704]{1,0:T(8,128)} %get-tuple-element.634, f32[512]{0:T(512)S(1)} %get-tuple-element.635), kind=kLoop, calls=%fused_computation.10.clone.1 | loop fusion | flops 8912384 | bytes 17829888 | tf_op jit(solution)/shard_map/while/body/eval_jaxpr/while/body/eval_jaxpr/reduce_sum | solution.py:58
  353.3 9.3 %fusion.45 = bf16[2,512,128]{2,1,0:T(8,128)(2,1)S(1)} fusion(bf16[2,512,128]{2,1,0:T(8,128)(2,1)S(1)} %get-tuple-element.646, s32[]{:T(128)} %get-tuple-element.645, bf16[8704,128]{1,0:T(8,128)(2,1)} %get-tuple-element.661, f32[512,8704]{1,0:T(8,128)} %get-tuple-element.634, f32[512]{0:T(512)S(1)} %get-tuple-element.635, f32[512]{0:T(512)S(1)} %fusion.44), kind=kOutput, calls=%fused_computation.17.clone.1 | convolution fusion | flops 1149894656 | bytes 20189188 | tf_op jit(solution)/shard_map/while/body/eval_jaxpr/while/body/eval_jaxpr/rk,kd->rd/dot_general | solution.py:59
  362.7 0.8 copy-done.5
  363.5 1.0 copy-done.1
  (41 shorter events, 0.4 us)
Async XLA Ops:
  0.0 5.8 %copy-start = (bf16[2,4096,128]{2,1,0:T(8,128)(2,1)S(1)}, bf16[2,4096,128]{2,1,0:T(8,128)(2,1)}, u32[]{:S(2)}) copy-start(bf16[2,4096,128]{2,1,0:T(8,128)(2,1)} %param.20) | copy-start | bytes 6291460
  17.4 54.6 %all-to-all-start = ((bf16[4,2,4,256,128]{4,3,2,1,0:T(8,128)(2,1)}), bf16[4,2,4,256,128]{4,3,2,1,0:T(8,128)(2,1)S(1)}, u32[]{:S(2)}, u32[]{:S(2)}) async-start(bf16[4,2,4,256,128]{4,3,2,1,0:T(8,128)(2,1)} %pad_maximum_fusion.4), calls=%async_computation | async-start | bytes 4194304 | tf_op jit(solution)/shard_map/all_to_all | solution.py:111
  71.9 52.4 %all-to-all-start.1 = ((bf16[2,16,256,128]{3,2,0,1:T(8,128)(2,1)}), bf16[2,16,256,128]{3,2,0,1:T(8,128)(2,1)}, u32[]{:S(2)}, u32[]{:S(2)}) async-start(bf16[2,16,256,128]{3,2,0,1:T(8,128)(2,1)} %copy.21), calls=%async_computation.1 | async-start | bytes 4194304 | tf_op jit(solution)/shard_map/all_to_all | solution.py:121
  80.6 47.5 %copy-start.3 = (bf16[2,256,128]{2,1,0:T(8,128)(2,1)S(1)}, bf16[2,256,128]{2,1,0:T(8,128)(2,1)}, u32[]{:S(2)}) copy-start(bf16[2,256,128]{2,1,0:T(8,128)(2,1)} %param.18) | copy-start | bytes 393220
  80.6 51.4 %copy-start.4 = (bf16[2,256,128]{2,1,0:T(8,128)(2,1)S(1)}, bf16[2,256,128]{2,1,0:T(8,128)(2,1)}, u32[]{:S(2)}) copy-start(bf16[2,256,128]{2,1,0:T(8,128)(2,1)} %param.17) | copy-start | bytes 393220
  80.6 78.2 %collective-permute-start = (bf16[2,16,256,128]{3,2,1,0:T(8,128)(2,1)S(1)}, bf16[2,16,256,128]{3,2,1,0:T(8,128)(2,1)}, u32[]{:S(2)}, u32[]{:S(2)}) collective-permute-start(bf16[2,16,256,128]{3,2,1,0:T(8,128)(2,1)S(1)} %bitcast.69), channel_id=1, source_target_pairs={{0,4},{4,0},{8,12},{12,8},{1,5},{5,1},{9,13},{13,9},{2,6},{6,2},{1... | collective-permute-start | bytes 6291464 | tf_op jit(solution)/shard_map/ppermute | solution.py:28
  128.0 73.9 %collective-permute-start.2 = (bf16[2,16,256,128]{3,2,1,0:T(8,128)(2,1)}, bf16[2,16,256,128]{3,2,1,0:T(8,128)(2,1)}, u32[]{:S(2)}, u32[]{:S(2)}) collective-permute-start(bf16[2,16,256,128]{3,2,1,0:T(8,128)(2,1)} %bitcast.71), channel_id=1, source_target_pairs={{0,4},{4,0},{8,12},{12,8},{1,5},{5,1},{9,13},{13,9},{2,6},{6,2},{1... | collective-permute-start | bytes 6291464 | tf_op jit(solution)/shard_map/ppermute | solution.py:28
  128.1 77.5 %collective-permute-start.3 = (bf16[2,256,128]{2,1,0:T(8,128)(2,1)S(1)}, bf16[2,256,128]{2,1,0:T(8,128)(2,1)S(1)}, u32[]{:S(2)}, u32[]{:S(2)}) collective-permute-start(bf16[2,256,128]{2,1,0:T(8,128)(2,1)S(1)} %copy-done.3), channel_id=1, source_target_pairs={{0,4},{4,8},{8,12},{1,5},{5,9},{9,13},{2,6},{6,10},{10,14},{3,7},{... | collective-permute-start | bytes 393224 | tf_op jit(solution)/shard_map/ppermute | solution.py:14
  132.0 83.9 %collective-permute-start.1 = (bf16[2,256,128]{2,1,0:T(8,128)(2,1)S(1)}, bf16[2,256,128]{2,1,0:T(8,128)(2,1)S(1)}, u32[]{:S(2)}, u32[]{:S(2)}) collective-permute-start(bf16[2,256,128]{2,1,0:T(8,128)(2,1)S(1)} %copy-done.4), channel_id=1, source_target_pairs={{0,4},{4,8},{8,12},{1,5},{5,9},{9,13},{2,6},{6,10},{10,14},{3,7},{... | collective-permute-start | bytes 393224 | tf_op jit(solution)/shard_map/ppermute | solution.py:14
  215.9 9.9 %copy-start.2 = (bf16[8,256,128]{2,1,0:T(8,128)(2,1)S(1)}, bf16[8,256,128]{2,1,0:T(8,128)(2,1)}, u32[]{:S(2)}) copy-start(bf16[8,256,128]{2,1,0:T(8,128)(2,1)} %param.16) | copy-start | bytes 1572868
  362.7 0.8 copy-start.5
  362.7 1.8 copy-start.1
